TPU v7x, 128 devices: a whole 4x4x4 slice. The times are simulated.
128 devices in a mesh: grid: 8 (over x, core), proc: 16 (over z, y).
Axes of the slice: x: 4, y: 4, z: 4, core: 2. Of those that a mesh axis runs over, the one named last changes fastest.
Arguments:
- rhs: float32 [3, 8, 16, 256, 1024], P(None, 'grid', 'proc'), may hold values from -6 to 6
- tile_pairs: int32 [2, 8, 16, 32], P(None, 'grid', 'proc'), may hold values from -1 to 31, as said below
- tiles: bfloat16 [2, 8, 16, 32, 256, 256], P(None, 'grid', 'proc'), may hold values from -0.09375 to 0.09375
- dinv: float32 [3, 8, 16, 256, 256], P(None, 'grid', 'proc'), as said below
Outputs:
- solution: float32 [3, 8, 16, 256, 1024], P(None, 'grid', 'proc')
Inputs may be any that keep to these rules, and one draw needn't show every extreme that they name: tile_pairs[t, g, p] holds distinct pair numbers in its first slots and -1 in the others; pair number q names block column q mod 16 and destination q // 16 (0: the same grid, 1: the partner grid). In every transition and grid one device uses all 32 slots and the others use 2 to 16 of them. Each dinv tile is lower triangular with diagonal entries between 0.5 and 1.4.
All inputs are finite; a program needn't handle non-finite values.
Results may differ from a plain program's by a relative error of at most 0.0021.
Values may be sent and summed in bfloat16 or wider, within the bound.
No kernel may reach another device: no remote copies, remote signals or barrier semaphores. Data moves between devices by JAX's collectives and lax.ppermute only.
A program may use at most 128 MiB of HBM per device.

v0:
```python
import jax
import jax.numpy as jnp
import numpy as np
from jax import lax
from jax.experimental import pallas as pl
from jax.experimental.pallas import tpu as pltpu
from jax.sharding import PartitionSpec as P

AXES = ("grid", "proc")
SIDE = 4
VM = 24
LINK = jnp.bfloat16
CHUNKS = (("y", 0, 256), ("z", 256, 256), ("y", 512, 256), ("z", 768, 256))


def ring_partner(place, flip):
    odd = place % 2
    return (place + 1 - 2 * (odd ^ flip)) % SIDE


def exchange_route(shape, axis, step):
    grids, procs = shape
    route = []
    for g in range(grids):
        for p in range(procs):
            z, y = divmod(p, SIDE)
            flip = (g + step) % 2
            if axis == "y":
                y = ring_partner(y, flip)
            else:
                z = ring_partner(z, flip)
            route.append((g * procs + p, g * procs + z * SIDE + y))
    return route


def gather_order(first, shape):
    grids, procs = shape
    table = np.zeros((grids * procs, procs), np.int32)
    for g in range(grids):
        for p in range(procs):

            def seq(t, flip=g % 2):
                near, far = ring_partner(t, flip), ring_partner(t, 1 - flip)
                return [t, near, far, ring_partner(far, flip)]

            z, y = divmod(p, SIDE)
            zs, ys = seq(z), seq(y)
            if first == "y":
                held = [a * SIDE + b for a in zs for b in ys]
            else:
                held = [a * SIDE + b for b in ys for a in zs]
            table[g * procs + p] = held
    return table


def gather_blocks(block, first, shape):
    held = block[None]
    for axis in (first, "z" if first == "y" else "y"):
        for step in (0, 1):
            got = lax.ppermute(held, AXES, exchange_route(shape, axis, step))
            held = jnp.concatenate([held, got])
    return held.reshape(-1, held.shape[-1])


def from_partner(block, shape, level):
    grids, procs = shape
    apart = 1 << level
    route = [(g * procs + p, (g ^ apart) * procs + p) for g in range(grids) for p in range(procs)]
    return lax.ppermute(block, AXES, route)


def table_kernel(level, where_ref, count_ref, tiles_ref, *refs):
    *out_refs, held, sem = refs
    count = count_ref[level]

    def copy(s):
        return pltpu.make_async_copy(tiles_ref.at[level, 0, 0, s], held.at[s], sem)

    def start(s, c):
        copy(s).start()
        return c

    def wait(s, c):
        copy(s).wait()
        return c

    lax.fori_loop(0, count, start, 0)
    lax.fori_loop(0, count, wait, 0)
    size = held.shape[1]
    for n, out_ref in enumerate(out_refs):
        kind, d = divmod(n, 2)
        blocks = out_ref.shape[1] // size
        for k in range(blocks):
            cols = pl.ds(k * size, size)
            slot = where_ref[level, kind, d * blocks + k]

            @pl.when(slot >= 0)
            def _():
                out_ref[:, cols] = held[jnp.maximum(slot, 0)]

            @pl.when(slot < 0)
            def _():
                out_ref[:, cols] = jnp.zeros((size, size), out_ref.dtype)


def build_tables(level, where, count, tiles):
    slots, size = tiles.shape[3:5]
    out = jax.ShapeDtypeStruct((size, slots // 2 * size), tiles.dtype)
    outs = pl.pallas_call(
        lambda *refs: table_kernel(level, *refs),
        out_shape=[out] * 4,
        in_specs=[
            pl.BlockSpec(memory_space=pltpu.SMEM),
            pl.BlockSpec(memory_space=pltpu.SMEM),
            pl.BlockSpec(memory_space=pl.ANY),
        ],
        out_specs=[pl.BlockSpec(memory_space=pltpu.VMEM)] * 4,
        scratch_shapes=[pltpu.VMEM(tiles.shape[3:], tiles.dtype), pltpu.SemaphoreType.DMA],
        compiler_params=pltpu.CompilerParams(vmem_limit_bytes=VM << 20),
        cost_estimate=pl.CostEstimate(flops=0, bytes_accessed=12 << 20, transcendentals=0),
    )(where, count, tiles)
    return {"y": outs[:2], "z": outs[2:]}


def diagonal_solve(factor, values):
    return jnp.dot(
        factor, values, precision=lax.Precision.HIGH, preferred_element_type=jnp.float32
    )


def make_body(shape):
    orders = [gather_order(first, shape) for first in ("y", "z")]

    def body(rhs, tile_pairs, tiles, dinv):
        levels = rhs.shape[0]
        rhs, dinv, pairs = rhs[:, 0, 0], dinv[:, 0, 0], tile_pairs[:, 0, 0]
        me = lax.axis_index("grid") * shape[1] + lax.axis_index("proc")
        held = jnp.stack([jnp.asarray(order)[me] for order in orders])
        wanted = jnp.concatenate([held, held + shape[1]], 1)
        hit = pairs[:, None, None, :] == wanted[None, :, :, None]
        index = lax.broadcasted_iota(jnp.int32, hit.shape, 3)
        where = jnp.max(jnp.where(hit, index, -1), -1)
        counts = jnp.sum((pairs >= 0).astype(jnp.int32), 1)
        tables = [build_tables(t, where, counts, tiles) for t in range(levels - 1)]
        solved = [[None] * len(CHUNKS) for _ in range(levels)]
        sent = [None] * len(CHUNKS)
        for c, (first, start, width) in enumerate(CHUNKS):
            now = diagonal_solve(dinv[0], rhs[0, :, start : start + width])
            solved[0][c], sent[c] = lax.optimization_barrier((now, now.astype(jnp.bfloat16)))
        for level in range(1, levels):
            kind = LINK if level == levels - 1 else jnp.float32
            for c, (first, start, width) in enumerate(CHUNKS):
                here, there = tables[level - 1][first]
                blocks = gather_blocks(sent[c], first, shape)
                away = jnp.dot(there, blocks, preferred_element_type=jnp.float32)
                away = from_partner(away.astype(kind), shape, level - 1)
                stay = jnp.dot(here, blocks, preferred_element_type=jnp.float32)
                stay = lax.optimization_barrier(
                    rhs[level, :, start : start + width] - stay
                )
                now = diagonal_solve(dinv[level], stay - away.astype(jnp.float32))
                if level < levels - 1:
                    now = lax.optimization_barrier((now, now.astype(jnp.bfloat16)))
                    solved[level][c], sent[c] = now
                else:
                    solved[level][c] = lax.optimization_barrier(now)
        out = jnp.stack([jnp.concatenate(row, 1) for row in solved])[:, None, None]
        return out

    return body


def solution(mesh):
    shape = (mesh.shape["grid"], mesh.shape["proc"])
    return jax.shard_map(
        make_body(shape),
        mesh=mesh,
        in_specs=(
            P(None, "grid", "proc", None, None),
            P(None, "grid", "proc", None),
            P(None, "grid", "proc", None, None, None),
            P(None, "grid", "proc", None, None),
        ),
        out_specs=P(None, "grid", "proc", None, None),
        check_vma=False,
    )
```

profile of v0, /device:TPU:0, one launch (start us, length us, event | category | flops | bytes accessed | tf_op | source)
XLA Modules:
  0.0 162.7 jit_solution(12989897232294709680)
XLA Ops:
  0.0 2.1 %fusion.47 = (bf16[256,256]{1,0:T(8,128)(2,1)S(1)}, f32[256,256]{1,0:T(8,128)}) fusion(f32[3,256,1024]{2,1,0:T(8,128)} %bitcast.219, f32[3,1,1,256,256]{4,3,2,1,0:T(8,128)} %param.9), kind=kOutput, calls=%fused_computation.153 | convolution fusion | flops 100728832 | bytes 917504 | tf_op jit(solution)/shard_map/dot_general | solution.py:126
  2.1 1.7 %collective-permute-start = (bf16[1,256,256]{2,1,0:T(8,128)(2,1)S(1)}, bf16[1,256,256]{2,1,0:T(8,128)(2,1)}, u32[]{:S(2)}, u32[]{:S(2)}) collective-permute-start(bf16[1,256,256]{2,1,0:T(8,128)(2,1)S(1)} %bitcast.199), channel_id=1, source_target_pairs={{0,1},{1,0},{2,3},{3,2},{4,5},{5,4},{6,7},{7,6},{8,9},{9,8},{10,11... | collective-permute-start | bytes 393224 | tf_op jit(solution)/shard_map/ppermute | solution.py:60
  3.8 2.0 %fusion.45 = (bf16[256,256]{1,0:T(8,128)(2,1)S(1)}, f32[256,256]{1,0:T(8,128)}) fusion(f32[3,256,1024]{2,1,0:T(8,128)} %bitcast.220, f32[3,1,1,256,256]{4,3,2,1,0:T(8,128)} %param.9), kind=kOutput, calls=%fused_computation.151 | convolution fusion | flops 100728832 | bytes 917504 | tf_op jit(solution)/shard_map/dot_general | solution.py:126
  5.8 1.9 %collective-permute-start.5 = (bf16[1,256,256]{2,1,0:T(8,128)(2,1)S(1)}, bf16[1,256,256]{2,1,0:T(8,128)(2,1)}, u32[]{:S(2)}, u32[]{:S(2)}) collective-permute-start(bf16[1,256,256]{2,1,0:T(8,128)(2,1)S(1)} %bitcast.195), channel_id=1, source_target_pairs={{0,4},{1,5},{2,6},{3,7},{4,0},{5,1},{6,2},{7,3},{8,12},{9,13},{10,... | collective-permute-start | bytes 393224 | tf_op jit(solution)/shard_map/ppermute | solution.py:60
  7.7 2.0 %fusion.43 = (bf16[256,256]{1,0:T(8,128)(2,1)S(1)}, f32[256,256]{1,0:T(8,128)}) fusion(f32[3,256,1024]{2,1,0:T(8,128)} %bitcast.221, f32[3,1,1,256,256]{4,3,2,1,0:T(8,128)} %param.9), kind=kOutput, calls=%fused_computation.149 | convolution fusion | flops 100728832 | bytes 917504 | tf_op jit(solution)/shard_map/dot_general | solution.py:126
  10.2 1.9 %fusion.41 = (bf16[256,256]{1,0:T(8,128)(2,1)S(1)}, f32[256,256]{1,0:T(8,128)}) fusion(f32[3,256,1024]{2,1,0:T(8,128)} %bitcast.222, f32[3,1,1,256,256]{4,3,2,1,0:T(8,128)S(1)} %copy-done.1), kind=kOutput, calls=%fused_computation.147 | convolution fusion | flops 100728832 | bytes 917504 | tf_op jit(solution)/shard_map/dot_general | solution.py:126
  16.6 3.4 %copy-done = bf16[2,1,1,32,256,256]{5,4,3,2,1,0:T(8,128)(2,1)S(1)} copy-done((bf16[2,1,1,32,256,256]{5,4,3,2,1,0:T(8,128)(2,1)S(1)}, bf16[2,1,1,32,256,256]{5,4,3,2,1,0:T(8,128)(2,1)}, u32[]{:S(2)}) %copy-start) | copy-done | bytes 8388632
  20.0 4.7 %shard_map.64 = (bf16[256,4096]{1,0:T(8,128)(2,1)S(1)}, bf16[256,4096]{1,0:T(8,128)(2,1)S(1)}, bf16[256,4096]{1,0:T(8,128)(2,1)S(1)}, bf16[256,4096]{1,0:T(8,128)(2,1)S(1)}) custom-call(s32[2,2,32]{2,1,0:T(2,128)S(1)} %select_reduce_fusion.refs_0_, s32[2]{0:T(128)S(1)} %fusion.40.refs_1_, bf16[2,1,1,32,256,256]{5,4,3,2,1,0:T(8,128)(2,1)S(1)} %copy-done), custom_call_target="tpu_custom_call" | custom-call | bytes 12582912 | tf_op jit(solution)/shard_map/pallas_call | solution.py:109
  24.7 3.0 %shard_map.65 = (bf16[256,4096]{1,0:T(8,128)(2,1)S(1)}, bf16[256,4096]{1,0:T(8,128)(2,1)S(1)}, bf16[256,4096]{1,0:T(8,128)(2,1)S(1)}, bf16[256,4096]{1,0:T(8,128)(2,1)S(1)}) custom-call(s32[2,2,32]{2,1,0:T(2,128)S(1)} %select_reduce_fusion.refs_0_, s32[2]{0:T(128)S(1)} %fusion.40.refs_1_, bf16[2,1,1,32,256,256]{5,4,3,2,1,0:T(8,128)(2,1)S(1)} %copy-done), custom_call_target="tpu_custom_call" | custom-call | bytes 12582912 | tf_op jit(solution)/shard_map/pallas_call | solution.py:109
  30.9 5.8 %collective-permute-start.6 = (bf16[2,256,256]{2,1,0:T(8,128)(2,1)S(1)}, bf16[2,256,256]{2,1,0:T(8,128)(2,1)S(1)}, u32[]{:S(2)}, u32[]{:S(2)}) collective-permute-start(bf16[2,256,256]{2,1,0:T(8,128)(2,1)S(1)} %pad_maximum_fusion.17), channel_id=1, source_target_pairs={{0,12},{1,13},{2,14},{3,15},{4,8},{5,9},{6,10},{7,11},{8,4},{9,5},... | collective-permute-start | bytes 786440 | tf_op jit(solution)/shard_map/ppermute | solution.py:60
  41.7 8.0 %collective-permute-start.2 = (bf16[4,256,256]{2,1,0:T(8,128)(2,1)S(1)}, bf16[4,256,256]{2,1,0:T(8,128)(2,1)S(1)}, u32[]{:S(2)}, u32[]{:S(2)}) collective-permute-start(bf16[4,256,256]{2,1,0:T(8,128)(2,1)S(1)} %pad_maximum_fusion.8), channel_id=1, source_target_pairs={{0,4},{1,5},{2,6},{3,7},{4,0},{5,1},{6,2},{7,3},{8,12},{9,13},{10,... | collective-permute-start | bytes 1572872 | tf_op jit(solution)/shard_map/ppermute | solution.py:60
  51.7 1.6 collective-permute-start.12
  53.3 2.1 %collective-permute-start.17 = (bf16[4,256,256]{2,1,0:T(8,128)(2,1)S(1)}, bf16[4,256,256]{2,1,0:T(8,128)(2,1)S(1)}, u32[]{:S(2)}, u32[]{:S(2)}) collective-permute-start(bf16[4,256,256]{2,1,0:T(8,128)(2,1)S(1)} %pad_maximum_fusion.11), channel_id=1, source_target_pairs={{0,1},{1,0},{2,3},{3,2},{4,5},{5,4},{6,7},{7,6},{8,9},{9,8},{10,11... | collective-permute-start | bytes 1572872 | tf_op jit(solution)/shard_map/ppermute | solution.py:60
  60.9 4.3 %collective-permute-start.8 = (bf16[8,256,256]{2,1,0:T(8,128)(2,1)S(1)}, bf16[8,256,256]{2,1,0:T(8,128)(2,1)S(1)}, u32[]{:S(2)}, u32[]{:S(2)}) collective-permute-start(bf16[8,256,256]{2,1,0:T(8,128)(2,1)S(1)} %pad_maximum_fusion.1), channel_id=1, source_target_pairs={{0,3},{1,2},{2,1},{3,0},{4,7},{5,6},{6,5},{7,4},{8,11},{9,10},{10,... | collective-permute-start | bytes 3145736 | tf_op jit(solution)/shard_map/ppermute | solution.py:60
  66.4 3.5 %collective-permute-start.13 = (bf16[8,256,256]{2,1,0:T(8,128)(2,1)S(1)}, bf16[8,256,256]{2,1,0:T(8,128)(2,1)S(1)}, u32[]{:S(2)}, u32[]{:S(2)}) collective-permute-start(bf16[8,256,256]{2,1,0:T(8,128)(2,1)S(1)} %pad_maximum_fusion.2), channel_id=1, source_target_pairs={{0,12},{1,13},{2,14},{3,15},{4,8},{5,9},{6,10},{7,11},{8,4},{9,5},... | collective-permute-start | bytes 3145736 | tf_op jit(solution)/shard_map/ppermute | solution.py:60
  70.0 5.4 %collective-permute-start.18 = (bf16[8,256,256]{2,1,0:T(8,128)(2,1)S(1)}, bf16[8,256,256]{2,1,0:T(8,128)(2,1)S(1)}, u32[]{:S(2)}, u32[]{:S(2)}) collective-permute-start(bf16[8,256,256]{2,1,0:T(8,128)(2,1)S(1)} %pad_maximum_fusion.3), channel_id=1, source_target_pairs={{0,3},{1,2},{2,1},{3,0},{4,7},{5,6},{6,5},{7,4},{8,11},{9,10},{10,... | collective-permute-start | bytes 3145736 | tf_op jit(solution)/shard_map/ppermute | solution.py:60
  79.0 6.2 %collective-permute-done.13 = bf16[8,256,256]{2,1,0:T(8,128)(2,1)S(1)} collective-permute-done((bf16[8,256,256]{2,1,0:T(8,128)(2,1)S(1)}, bf16[8,256,256]{2,1,0:T(8,128)(2,1)S(1)}, u32[]{:S(2)}, u32[]{:S(2)}) %collective-permute-start.13) | collective-permute-done | bytes 1048608 | tf_op jit(solution)/shard_map/ppermute | solution.py:60
  93.2 1.6 collective-permute-start.25
  94.9 2.1 %collective-permute-start.30 = (bf16[1,256,256]{2,1,0:T(8,128)(2,1)S(1)}, bf16[1,256,256]{2,1,0:T(8,128)(2,1)S(1)}, u32[]{:S(2)}, u32[]{:S(2)}) collective-permute-start(bf16[1,256,256]{2,1,0:T(8,128)(2,1)S(1)} %bitcast.207), channel_id=1, source_target_pairs={{0,1},{1,0},{2,3},{3,2},{4,5},{5,4},{6,7},{7,6},{8,9},{9,8},{10,11... | collective-permute-start | bytes 393224 | tf_op jit(solution)/shard_map/ppermute | solution.py:60
  98.2 3.8 %collective-permute-start.21 = (bf16[2,256,256]{2,1,0:T(8,128)(2,1)S(1)}, bf16[2,256,256]{2,1,0:T(8,128)(2,1)S(1)}, u32[]{:S(2)}, u32[]{:S(2)}) collective-permute-start(bf16[2,256,256]{2,1,0:T(8,128)(2,1)S(1)} %pad_maximum_fusion.20), channel_id=1, source_target_pairs={{0,3},{1,2},{2,1},{3,0},{4,7},{5,6},{6,5},{7,4},{8,11},{9,10},{10,... | collective-permute-start | bytes 786440 | tf_op jit(solution)/shard_map/ppermute | solution.py:60
  103.5 2.2 %collective-permute-start.36 = (bf16[2,256,256]{2,1,0:T(8,128)(2,1)S(1)}, bf16[2,256,256]{2,1,0:T(8,128)(2,1)S(1)}, u32[]{:S(2)}, u32[]{:S(2)}) collective-permute-start(bf16[2,256,256]{2,1,0:T(8,128)(2,1)S(1)} %pad_maximum_fusion.23), channel_id=1, source_target_pairs={{0,12},{1,13},{2,14},{3,15},{4,8},{5,9},{6,10},{7,11},{8,4},{9,5},... | collective-permute-start | bytes 786440 | tf_op jit(solution)/shard_map/ppermute | solution.py:60
  107.6 2.3 %collective-permute-done.26 = bf16[2,256,256]{2,1,0:T(8,128)(2,1)S(1)} collective-permute-done((bf16[2,256,256]{2,1,0:T(8,128)(2,1)S(1)}, bf16[2,256,256]{2,1,0:T(8,128)(2,1)S(1)}, u32[]{:S(2)}, u32[]{:S(2)}) %collective-permute-start.26) | collective-permute-done | bytes 262176 | tf_op jit(solution)/shard_map/ppermute | solution.py:60
  111.4 4.1 %collective-permute-done.36 = bf16[2,256,256]{2,1,0:T(8,128)(2,1)S(1)} collective-permute-done((bf16[2,256,256]{2,1,0:T(8,128)(2,1)S(1)}, bf16[2,256,256]{2,1,0:T(8,128)(2,1)S(1)}, u32[]{:S(2)}, u32[]{:S(2)}) %collective-permute-start.36) | collective-permute-done | bytes 262176 | tf_op jit(solution)/shard_map/ppermute | solution.py:60
  116.0 1.7 %collective-permute-start.23 = (bf16[8,256,256]{2,1,0:T(8,128)(2,1)S(1)}, bf16[8,256,256]{2,1,0:T(8,128)(2,1)S(1)}, u32[]{:S(2)}, u32[]{:S(2)}) collective-permute-start(bf16[8,256,256]{2,1,0:T(8,128)(2,1)S(1)} %pad_maximum_fusion.4), channel_id=1, source_target_pairs={{0,12},{1,13},{2,14},{3,15},{4,8},{5,9},{6,10},{7,11},{8,4},{9,5},... | collective-permute-start | bytes 3145736 | tf_op jit(solution)/shard_map/ppermute | solution.py:60
  120.3 1.9 %collective-permute-done.32 = bf16[4,256,256]{2,1,0:T(8,128)(2,1)S(1)} collective-permute-done((bf16[4,256,256]{2,1,0:T(8,128)(2,1)S(1)}, bf16[4,256,256]{2,1,0:T(8,128)(2,1)S(1)}, u32[]{:S(2)}, u32[]{:S(2)}) %collective-permute-start.32) | collective-permute-done | bytes 524320 | tf_op jit(solution)/shard_map/ppermute | solution.py:60
  122.3 2.1 %collective-permute-start.33 = (bf16[8,256,256]{2,1,0:T(8,128)(2,1)S(1)}, bf16[8,256,256]{2,1,0:T(8,128)(2,1)S(1)}, u32[]{:S(2)}, u32[]{:S(2)}) collective-permute-start(bf16[8,256,256]{2,1,0:T(8,128)(2,1)S(1)} %pad_maximum_fusion.6), channel_id=1, source_target_pairs={{0,12},{1,13},{2,14},{3,15},{4,8},{5,9},{6,10},{7,11},{8,4},{9,5},... | collective-permute-start | bytes 3145736 | tf_op jit(solution)/shard_map/ppermute | solution.py:60
  124.4 4.3 %collective-permute-done.37 = bf16[4,256,256]{2,1,0:T(8,128)(2,1)S(1)} collective-permute-done((bf16[4,256,256]{2,1,0:T(8,128)(2,1)S(1)}, bf16[4,256,256]{2,1,0:T(8,128)(2,1)S(1)}, u32[]{:S(2)}, u32[]{:S(2)}) %collective-permute-start.37) | collective-permute-done | bytes 524320 | tf_op jit(solution)/shard_map/ppermute | solution.py:60
  129.2 5.7 %collective-permute-done.23 = bf16[8,256,256]{2,1,0:T(8,128)(2,1)S(1)} collective-permute-done((bf16[8,256,256]{2,1,0:T(8,128)(2,1)S(1)}, bf16[8,256,256]{2,1,0:T(8,128)(2,1)S(1)}, u32[]{:S(2)}, u32[]{:S(2)}) %collective-permute-start.23) | collective-permute-done | bytes 1048608 | tf_op jit(solution)/shard_map/ppermute | solution.py:60
  136.1 10.1 %collective-permute-done.33 = bf16[8,256,256]{2,1,0:T(8,128)(2,1)S(1)} collective-permute-done((bf16[8,256,256]{2,1,0:T(8,128)(2,1)S(1)}, bf16[8,256,256]{2,1,0:T(8,128)(2,1)S(1)}, u32[]{:S(2)}, u32[]{:S(2)}) %collective-permute-start.33) | collective-permute-done | bytes 1048608 | tf_op jit(solution)/shard_map/ppermute | solution.py:60
  151.6 2.0 %collective-permute-start.34 = (bf16[256,256]{1,0:T(8,128)(2,1)S(1)}, bf16[256,256]{1,0:T(8,128)(2,1)S(1)}, u32[]{:S(2)}, u32[]{:S(2)}) collective-permute-start(bf16[256,256]{1,0:T(8,128)(2,1)S(1)} %convolution_convert_fusion.1), channel_id=1, source_target_pairs={{0,32},{1,33},{2,34},{3,35},{4,36},{5,37},{6,38},{7,39},{8,40},{9,... | collective-permute-start | bytes 393224 | tf_op jit(solution)/shard_map/ppermute | solution.py:69
  154.0 3.6 %collective-permute-done.29 = bf16[256,256]{1,0:T(8,128)(2,1)S(1)} collective-permute-done((bf16[256,256]{1,0:T(8,128)(2,1)S(1)}, bf16[256,256]{1,0:T(8,128)(2,1)S(1)}, u32[]{:S(2)}, u32[]{:S(2)}) %collective-permute-start.29) | collective-permute-done | bytes 131104 | tf_op jit(solution)/shard_map/ppermute | solution.py:69
  160.8 1.9 %maximum_bitcast_fusion = f32[3,1,1,256,1024]{4,3,2,1,0:T(8,128)} fusion(f32[1,256,1024]{2,1,0:T(8,128)S(1)} %maximum_bitcast_fusion.3, f32[1,256,1024]{2,1,0:T(8,128)S(1)} %maximum_bitcast_fusion.2, f32[1,256,1024]{2,1,0:T(8,128)S(1)} %maximum_bitcast_fusion.1), kind=kLoop, calls=%fused_computation | loop fusion | flops 1572864 | bytes 6291456 | tf_op jit(solution)/shard_map/broadcast_in_dim | solution.py:167
  (165 shorter events, 52.8 us)
Async XLA Ops:
  2.1 25.6 %collective-permute-start = (bf16[1,256,256]{2,1,0:T(8,128)(2,1)S(1)}, bf16[1,256,256]{2,1,0:T(8,128)(2,1)}, u32[]{:S(2)}, u32[]{:S(2)}) collective-permute-start(bf16[1,256,256]{2,1,0:T(8,128)(2,1)S(1)} %bitcast.199), channel_id=1, source_target_pairs={{0,1},{1,0},{2,3},{3,2},{4,5},{5,4},{6,7},{7,6},{8,9},{9,8},{10,11... | collective-permute-start | bytes 393224 | tf_op jit(solution)/shard_map/ppermute | solution.py:60
  5.8 24.2 %collective-permute-start.5 = (bf16[1,256,256]{2,1,0:T(8,128)(2,1)S(1)}, bf16[1,256,256]{2,1,0:T(8,128)(2,1)}, u32[]{:S(2)}, u32[]{:S(2)}) collective-permute-start(bf16[1,256,256]{2,1,0:T(8,128)(2,1)S(1)} %bitcast.195), channel_id=1, source_target_pairs={{0,4},{1,5},{2,6},{3,7},{4,0},{5,1},{6,2},{7,3},{8,12},{9,13},{10,... | collective-permute-start | bytes 393224 | tf_op jit(solution)/shard_map/ppermute | solution.py:60
  9.7 27.0 %collective-permute-start.10 = (bf16[1,256,256]{2,1,0:T(8,128)(2,1)S(1)}, bf16[1,256,256]{2,1,0:T(8,128)(2,1)}, u32[]{:S(2)}, u32[]{:S(2)}) collective-permute-start(bf16[1,256,256]{2,1,0:T(8,128)(2,1)S(1)} %bitcast.191), channel_id=1, source_target_pairs={{0,1},{1,0},{2,3},{3,2},{4,5},{5,4},{6,7},{7,6},{8,9},{9,8},{10,11... | collective-permute-start | bytes 393224 | tf_op jit(solution)/shard_map/ppermute | solution.py:60
  12.1 25.6 %collective-permute-start.15 = (bf16[1,256,256]{2,1,0:T(8,128)(2,1)S(1)}, bf16[1,256,256]{2,1,0:T(8,128)(2,1)S(1)}, u32[]{:S(2)}, u32[]{:S(2)}) collective-permute-start(bf16[1,256,256]{2,1,0:T(8,128)(2,1)S(1)} %bitcast.187), channel_id=1, source_target_pairs={{0,4},{1,5},{2,6},{3,7},{4,0},{5,1},{6,2},{7,3},{8,12},{9,13},{10,... | collective-permute-start | bytes 393224 | tf_op jit(solution)/shard_map/ppermute | solution.py:60
  28.8 11.9 %collective-permute-start.1 = (bf16[2,256,256]{2,1,0:T(8,128)(2,1)S(1)}, bf16[2,256,256]{2,1,0:T(8,128)(2,1)S(1)}, u32[]{:S(2)}, u32[]{:S(2)}) collective-permute-start(bf16[2,256,256]{2,1,0:T(8,128)(2,1)S(1)} %pad_maximum_fusion.16), channel_id=1, source_target_pairs={{0,3},{1,2},{2,1},{3,0},{4,7},{5,6},{6,5},{7,4},{8,11},{9,10},{10,... | collective-permute-start | bytes 786440 | tf_op jit(solution)/shard_map/ppermute | solution.py:60
  30.9 18.7 %collective-permute-start.6 = (bf16[2,256,256]{2,1,0:T(8,128)(2,1)S(1)}, bf16[2,256,256]{2,1,0:T(8,128)(2,1)S(1)}, u32[]{:S(2)}, u32[]{:S(2)}) collective-permute-start(bf16[2,256,256]{2,1,0:T(8,128)(2,1)S(1)} %pad_maximum_fusion.17), channel_id=1, source_target_pairs={{0,12},{1,13},{2,14},{3,15},{4,8},{5,9},{6,10},{7,11},{8,4},{9,5},... | collective-permute-start | bytes 786440 | tf_op jit(solution)/shard_map/ppermute | solution.py:60
  37.7 13.0 %collective-permute-start.11 = (bf16[2,256,256]{2,1,0:T(8,128)(2,1)S(1)}, bf16[2,256,256]{2,1,0:T(8,128)(2,1)S(1)}, u32[]{:S(2)}, u32[]{:S(2)}) collective-permute-start(bf16[2,256,256]{2,1,0:T(8,128)(2,1)S(1)} %pad_maximum_fusion.18), channel_id=1, source_target_pairs={{0,3},{1,2},{2,1},{3,0},{4,7},{5,6},{6,5},{7,4},{8,11},{9,10},{10,... | collective-permute-start | bytes 786440 | tf_op jit(solution)/shard_map/ppermute | solution.py:60
  37.8 15.5 %collective-permute-start.16 = (bf16[2,256,256]{2,1,0:T(8,128)(2,1)S(1)}, bf16[2,256,256]{2,1,0:T(8,128)(2,1)S(1)}, u32[]{:S(2)}, u32[]{:S(2)}) collective-permute-start(bf16[2,256,256]{2,1,0:T(8,128)(2,1)S(1)} %pad_maximum_fusion.19), channel_id=1, source_target_pairs={{0,12},{1,13},{2,14},{3,15},{4,8},{5,9},{6,10},{7,11},{8,4},{9,5},... | collective-permute-start | bytes 786440 | tf_op jit(solution)/shard_map/ppermute | solution.py:60
  41.7 15.1 %collective-permute-start.2 = (bf16[4,256,256]{2,1,0:T(8,128)(2,1)S(1)}, bf16[4,256,256]{2,1,0:T(8,128)(2,1)S(1)}, u32[]{:S(2)}, u32[]{:S(2)}) collective-permute-start(bf16[4,256,256]{2,1,0:T(8,128)(2,1)S(1)} %pad_maximum_fusion.8), channel_id=1, source_target_pairs={{0,4},{1,5},{2,6},{3,7},{4,0},{5,1},{6,2},{7,3},{8,12},{9,13},{10,... | collective-permute-start | bytes 1572872 | tf_op jit(solution)/shard_map/ppermute | solution.py:60
  50.6 9.3 %collective-permute-start.7 = (bf16[4,256,256]{2,1,0:T(8,128)(2,1)S(1)}, bf16[4,256,256]{2,1,0:T(8,128)(2,1)S(1)}, u32[]{:S(2)}, u32[]{:S(2)}) collective-permute-start(bf16[4,256,256]{2,1,0:T(8,128)(2,1)S(1)} %pad_maximum_fusion.9), channel_id=1, source_target_pairs={{0,1},{1,0},{2,3},{3,2},{4,5},{5,4},{6,7},{7,6},{8,9},{9,8},{10,11... | collective-permute-start | bytes 1572872 | tf_op jit(solution)/shard_map/ppermute | solution.py:60
  51.7 13.7 %collective-permute-start.12 = (bf16[4,256,256]{2,1,0:T(8,128)(2,1)S(1)}, bf16[4,256,256]{2,1,0:T(8,128)(2,1)S(1)}, u32[]{:S(2)}, u32[]{:S(2)}) collective-permute-start(bf16[4,256,256]{2,1,0:T(8,128)(2,1)S(1)} %pad_maximum_fusion.10), channel_id=1, source_target_pairs={{0,4},{1,5},{2,6},{3,7},{4,0},{5,1},{6,2},{7,3},{8,12},{9,13},{10,... | collective-permute-start | bytes 1572872 | tf_op jit(solution)/shard_map/ppermute | solution.py:60
  53.3 16.6 %collective-permute-start.17 = (bf16[4,256,256]{2,1,0:T(8,128)(2,1)S(1)}, bf16[4,256,256]{2,1,0:T(8,128)(2,1)S(1)}, u32[]{:S(2)}, u32[]{:S(2)}) collective-permute-start(bf16[4,256,256]{2,1,0:T(8,128)(2,1)S(1)} %pad_maximum_fusion.11), channel_id=1, source_target_pairs={{0,1},{1,0},{2,3},{3,2},{4,5},{5,4},{6,7},{7,6},{8,9},{9,8},{10,11... | collective-permute-start | bytes 1572872 | tf_op jit(solution)/shard_map/ppermute | solution.py:60
  57.8 17.8 %collective-permute-start.3 = (bf16[8,256,256]{2,1,0:T(8,128)(2,1)S(1)}, bf16[8,256,256]{2,1,0:T(8,128)(2,1)S(1)}, u32[]{:S(2)}, u32[]{:S(2)}) collective-permute-start(bf16[8,256,256]{2,1,0:T(8,128)(2,1)S(1)} %pad_maximum_fusion), channel_id=1, source_target_pairs={{0,12},{1,13},{2,14},{3,15},{4,8},{5,9},{6,10},{7,11},{8,4},{9,5},... | collective-permute-start | bytes 3145736 | tf_op jit(solution)/shard_map/ppermute | solution.py:60
  60.9 17.0 %collective-permute-start.8 = (bf16[8,256,256]{2,1,0:T(8,128)(2,1)S(1)}, bf16[8,256,256]{2,1,0:T(8,128)(2,1)S(1)}, u32[]{:S(2)}, u32[]{:S(2)}) collective-permute-start(bf16[8,256,256]{2,1,0:T(8,128)(2,1)S(1)} %pad_maximum_fusion.1), channel_id=1, source_target_pairs={{0,3},{1,2},{2,1},{3,0},{4,7},{5,6},{6,5},{7,4},{8,11},{9,10},{10,... | collective-permute-start | bytes 3145736 | tf_op jit(solution)/shard_map/ppermute | solution.py:60
  66.4 18.8 %collective-permute-start.13 = (bf16[8,256,256]{2,1,0:T(8,128)(2,1)S(1)}, bf16[8,256,256]{2,1,0:T(8,128)(2,1)S(1)}, u32[]{:S(2)}, u32[]{:S(2)}) collective-permute-start(bf16[8,256,256]{2,1,0:T(8,128)(2,1)S(1)} %pad_maximum_fusion.2), channel_id=1, source_target_pairs={{0,12},{1,13},{2,14},{3,15},{4,8},{5,9},{6,10},{7,11},{8,4},{9,5},... | collective-permute-start | bytes 3145736 | tf_op jit(solution)/shard_map/ppermute | solution.py:60
  70.0 19.2 %collective-permute-start.18 = (bf16[8,256,256]{2,1,0:T(8,128)(2,1)S(1)}, bf16[8,256,256]{2,1,0:T(8,128)(2,1)S(1)}, u32[]{:S(2)}, u32[]{:S(2)}) collective-permute-start(bf16[8,256,256]{2,1,0:T(8,128)(2,1)S(1)} %pad_maximum_fusion.3), channel_id=1, source_target_pairs={{0,3},{1,2},{2,1},{3,0},{4,7},{5,6},{6,5},{7,4},{8,11},{9,10},{10,... | collective-permute-start | bytes 3145736 | tf_op jit(solution)/shard_map/ppermute | solution.py:60
  76.4 15.0 %collective-permute-start.4 = (f32[256,256]{1,0:T(8,128)S(1)}, f32[256,256]{1,0:T(8,128)S(1)}, u32[]{:S(2)}, u32[]{:S(2)}) collective-permute-start(f32[256,256]{1,0:T(8,128)S(1)} %fusion.49), channel_id=1, source_target_pairs={{0,16},{1,17},{2,18},{3,19},{4,20},{5,21},{6,22},{7,23},{8,24},{9,... | collective-permute-start | bytes 786440 | tf_op jit(solution)/shard_map/ppermute | solution.py:69
  78.7 13.0 %collective-permute-start.9 = (f32[256,256]{1,0:T(8,128)S(1)}, f32[256,256]{1,0:T(8,128)S(1)}, u32[]{:S(2)}, u32[]{:S(2)}) collective-permute-start(f32[256,256]{1,0:T(8,128)S(1)} %fusion.50), channel_id=1, source_target_pairs={{0,16},{1,17},{2,18},{3,19},{4,20},{5,21},{6,22},{7,23},{8,24},{9,... | collective-permute-start | bytes 786440 | tf_op jit(solution)/shard_map/ppermute | solution.py:69
  93.2 8.8 %collective-permute-start.25 = (bf16[1,256,256]{2,1,0:T(8,128)(2,1)S(1)}, bf16[1,256,256]{2,1,0:T(8,128)(2,1)S(1)}, u32[]{:S(2)}, u32[]{:S(2)}) collective-permute-start(bf16[1,256,256]{2,1,0:T(8,128)(2,1)S(1)} %bitcast.211), channel_id=1, source_target_pairs={{0,4},{1,5},{2,6},{3,7},{4,0},{5,1},{6,2},{7,3},{8,12},{9,13},{10,... | collective-permute-start | bytes 393224 | tf_op jit(solution)/shard_map/ppermute | solution.py:60
  94.9 8.2 %collective-permute-start.30 = (bf16[1,256,256]{2,1,0:T(8,128)(2,1)S(1)}, bf16[1,256,256]{2,1,0:T(8,128)(2,1)S(1)}, u32[]{:S(2)}, u32[]{:S(2)}) collective-permute-start(bf16[1,256,256]{2,1,0:T(8,128)(2,1)S(1)} %bitcast.207), channel_id=1, source_target_pairs={{0,1},{1,0},{2,3},{3,2},{4,5},{5,4},{6,7},{7,6},{8,9},{9,8},{10,11... | collective-permute-start | bytes 393224 | tf_op jit(solution)/shard_map/ppermute | solution.py:60
  98.2 8.2 %collective-permute-start.21 = (bf16[2,256,256]{2,1,0:T(8,128)(2,1)S(1)}, bf16[2,256,256]{2,1,0:T(8,128)(2,1)S(1)}, u32[]{:S(2)}, u32[]{:S(2)}) collective-permute-start(bf16[2,256,256]{2,1,0:T(8,128)(2,1)S(1)} %pad_maximum_fusion.20), channel_id=1, source_target_pairs={{0,3},{1,2},{2,1},{3,0},{4,7},{5,6},{6,5},{7,4},{8,11},{9,10},{10,... | collective-permute-start | bytes 786440 | tf_op jit(solution)/shard_map/ppermute | solution.py:60
  102.1 7.9 %collective-permute-start.26 = (bf16[2,256,256]{2,1,0:T(8,128)(2,1)S(1)}, bf16[2,256,256]{2,1,0:T(8,128)(2,1)S(1)}, u32[]{:S(2)}, u32[]{:S(2)}) collective-permute-start(bf16[2,256,256]{2,1,0:T(8,128)(2,1)S(1)} %pad_maximum_fusion.21), channel_id=1, source_target_pairs={{0,12},{1,13},{2,14},{3,15},{4,8},{5,9},{6,10},{7,11},{8,4},{9,5},... | collective-permute-start | bytes 786440 | tf_op jit(solution)/shard_map/ppermute | solution.py:60
  103.5 12.1 %collective-permute-start.36 = (bf16[2,256,256]{2,1,0:T(8,128)(2,1)S(1)}, bf16[2,256,256]{2,1,0:T(8,128)(2,1)S(1)}, u32[]{:S(2)}, u32[]{:S(2)}) collective-permute-start(bf16[2,256,256]{2,1,0:T(8,128)(2,1)S(1)} %pad_maximum_fusion.23), channel_id=1, source_target_pairs={{0,12},{1,13},{2,14},{3,15},{4,8},{5,9},{6,10},{7,11},{8,4},{9,5},... | collective-permute-start | bytes 786440 | tf_op jit(solution)/shard_map/ppermute | solution.py:60
  106.4 9.4 %collective-permute-start.22 = (bf16[4,256,256]{2,1,0:T(8,128)(2,1)S(1)}, bf16[4,256,256]{2,1,0:T(8,128)(2,1)S(1)}, u32[]{:S(2)}, u32[]{:S(2)}) collective-permute-start(bf16[4,256,256]{2,1,0:T(8,128)(2,1)S(1)} %pad_maximum_fusion.12), channel_id=1, source_target_pairs={{0,4},{1,5},{2,6},{3,7},{4,0},{5,1},{6,2},{7,3},{8,12},{9,13},{10,... | collective-permute-start | bytes 1572872 | tf_op jit(solution)/shard_map/ppermute | solution.py:60
  110.0 9.3 %collective-permute-start.27 = (bf16[4,256,256]{2,1,0:T(8,128)(2,1)S(1)}, bf16[4,256,256]{2,1,0:T(8,128)(2,1)S(1)}, u32[]{:S(2)}, u32[]{:S(2)}) collective-permute-start(bf16[4,256,256]{2,1,0:T(8,128)(2,1)S(1)} %pad_maximum_fusion.13), channel_id=1, source_target_pairs={{0,1},{1,0},{2,3},{3,2},{4,5},{5,4},{6,7},{7,6},{8,9},{9,8},{10,11... | collective-permute-start | bytes 1572872 | tf_op jit(solution)/shard_map/ppermute | solution.py:60
  110.8 11.4 %collective-permute-start.32 = (bf16[4,256,256]{2,1,0:T(8,128)(2,1)S(1)}, bf16[4,256,256]{2,1,0:T(8,128)(2,1)S(1)}, u32[]{:S(2)}, u32[]{:S(2)}) collective-permute-start(bf16[4,256,256]{2,1,0:T(8,128)(2,1)S(1)} %pad_maximum_fusion.14), channel_id=1, source_target_pairs={{0,4},{1,5},{2,6},{3,7},{4,0},{5,1},{6,2},{7,3},{8,12},{9,13},{10,... | collective-permute-start | bytes 1572872 | tf_op jit(solution)/shard_map/ppermute | solution.py:60
  115.6 13.1 %collective-permute-start.37 = (bf16[4,256,256]{2,1,0:T(8,128)(2,1)S(1)}, bf16[4,256,256]{2,1,0:T(8,128)(2,1)S(1)}, u32[]{:S(2)}, u32[]{:S(2)}) collective-permute-start(bf16[4,256,256]{2,1,0:T(8,128)(2,1)S(1)} %pad_maximum_fusion.15), channel_id=1, source_target_pairs={{0,1},{1,0},{2,3},{3,2},{4,5},{5,4},{6,7},{7,6},{8,9},{9,8},{10,11... | collective-permute-start | bytes 1572872 | tf_op jit(solution)/shard_map/ppermute | solution.py:60
  116.0 19.0 %collective-permute-start.23 = (bf16[8,256,256]{2,1,0:T(8,128)(2,1)S(1)}, bf16[8,256,256]{2,1,0:T(8,128)(2,1)S(1)}, u32[]{:S(2)}, u32[]{:S(2)}) collective-permute-start(bf16[8,256,256]{2,1,0:T(8,128)(2,1)S(1)} %pad_maximum_fusion.4), channel_id=1, source_target_pairs={{0,12},{1,13},{2,14},{3,15},{4,8},{5,9},{6,10},{7,11},{8,4},{9,5},... | collective-permute-start | bytes 3145736 | tf_op jit(solution)/shard_map/ppermute | solution.py:60
  119.4 27.7 %collective-permute-start.28 = (bf16[8,256,256]{2,1,0:T(8,128)(2,1)S(1)}, bf16[8,256,256]{2,1,0:T(8,128)(2,1)S(1)}, u32[]{:S(2)}, u32[]{:S(2)}) collective-permute-start(bf16[8,256,256]{2,1,0:T(8,128)(2,1)S(1)} %pad_maximum_fusion.5), channel_id=1, source_target_pairs={{0,3},{1,2},{2,1},{3,0},{4,7},{5,6},{6,5},{7,4},{8,11},{9,10},{10,... | collective-permute-start | bytes 3145736 | tf_op jit(solution)/shard_map/ppermute | solution.py:60
  122.3 23.9 %collective-permute-start.33 = (bf16[8,256,256]{2,1,0:T(8,128)(2,1)S(1)}, bf16[8,256,256]{2,1,0:T(8,128)(2,1)S(1)}, u32[]{:S(2)}, u32[]{:S(2)}) collective-permute-start(bf16[8,256,256]{2,1,0:T(8,128)(2,1)S(1)} %pad_maximum_fusion.6), channel_id=1, source_target_pairs={{0,12},{1,13},{2,14},{3,15},{4,8},{5,9},{6,10},{7,11},{8,4},{9,5},... | collective-permute-start | bytes 3145736 | tf_op jit(solution)/shard_map/ppermute | solution.py:60
  128.8 21.1 %collective-permute-start.38 = (bf16[8,256,256]{2,1,0:T(8,128)(2,1)S(1)}, bf16[8,256,256]{2,1,0:T(8,128)(2,1)S(1)}, u32[]{:S(2)}, u32[]{:S(2)}) collective-permute-start(bf16[8,256,256]{2,1,0:T(8,128)(2,1)S(1)} %pad_maximum_fusion.7), channel_id=1, source_target_pairs={{0,3},{1,2},{2,1},{3,0},{4,7},{5,6},{6,5},{7,4},{8,11},{9,10},{10,... | collective-permute-start | bytes 3145736 | tf_op jit(solution)/shard_map/ppermute | solution.py:60
  135.8 17.9 %collective-permute-start.24 = (bf16[256,256]{1,0:T(8,128)(2,1)S(1)}, bf16[256,256]{1,0:T(8,128)(2,1)S(1)}, u32[]{:S(2)}, u32[]{:S(2)}) collective-permute-start(bf16[256,256]{1,0:T(8,128)(2,1)S(1)} %convolution_convert_fusion.3), channel_id=1, source_target_pairs={{0,32},{1,33},{2,34},{3,35},{4,36},{5,37},{6,38},{7,39},{8,40},{9,... | collective-permute-start | bytes 393224 | tf_op jit(solution)/shard_map/ppermute | solution.py:69
  (15 other events, 104.4 us)
where the time goes:
time: 164 us; the launch traced here: 163 us
  starting transfers between devices  59.1 us (36%)
  waiting for transfers between devices  48.7 us (30%)
  matrix products  21.7 us (13%)
  other arithmetic  13.6 us (8%)
  local copies, waits for them, and re-layouts  11.1 us (7%)
  Pallas kernels  7.74 us (5%)
    ppermute x32, starting transfers between devices, gather_blocks(): got = lax.ppermute(held, AXES, exchange_route(shape, axis, step))  55.6 us
    ppermute x32, waiting for transfers between devices, gather_blocks(): got = lax.ppermute(held, AXES, exchange_route(shape, axis, step))  42.4 us
    dot_general x12, matrix products, diagonal_solve(): jnp.dot(factor, values, precision=lax.Precision.HIGH, preferred_element_t...  10.3 us
    unnamed x46, local copies, waits for them, and re-layouts  9.84 us
    concatenate x24, other arithmetic, gather_blocks(): held = jnp.concatenate([held, got])  9.75 us
    pallas_call x2, Pallas kernels, build_tables(): pl.pallas_call(lambda *refs: table_kernel(level, *refs), out_shape=[out]...  7.74 us
    ppermute x8, waiting for transfers between devices, from_partner(): return lax.ppermute(block, AXES, route)  6.37 us
    dot_general x8, matrix products, body(): away = jnp.dot(there, blocks, preferred_element_type=jnp.float32)  5.69 us
  transfers between devices with their start and end apart: 40, of which 21 were waited for; matrix products, arithmetic and copies ran while one was open for 23% of the time, Pallas kernels for 5%

commit v1 on v0

--- a/solution.py
+++ b/solution.py
@@ -8,7 +8,7 @@
 
 AXES = ("grid", "proc")
 SIDE = 4
-VM = 24
+VM = 13
 LINK = jnp.bfloat16
 CHUNKS = (("y", 0, 256), ("z", 256, 256), ("y", 512, 256), ("z", 768, 256))
 
@@ -54,12 +54,13 @@
 
 
 def gather_blocks(block, first, shape):
-    held = block[None]
+    held, got = block[None], None
     for axis in (first, "z" if first == "y" else "y"):
         for step in (0, 1):
+            if got is not None:
+                held = lax.optimization_barrier(jnp.concatenate([held, got]))
             got = lax.ppermute(held, AXES, exchange_route(shape, axis, step))
-            held = jnp.concatenate([held, got])
-    return held.reshape(-1, held.shape[-1])
+    return [blocks.reshape(-1, blocks.shape[-1]) for blocks in (held, got)]
 
 
 def from_partner(block, shape, level):
@@ -87,39 +88,44 @@
     lax.fori_loop(0, count, start, 0)
     lax.fori_loop(0, count, wait, 0)
     size = held.shape[1]
-    for n, out_ref in enumerate(out_refs):
-        kind, d = divmod(n, 2)
-        blocks = out_ref.shape[1] // size
-        for k in range(blocks):
-            cols = pl.ds(k * size, size)
-            slot = where_ref[level, kind, d * blocks + k]
+    for kind in range(len(out_refs) // 3):
+        own_ref, here_ref, there_ref = out_refs[3 * kind : 3 * kind + 3]
+        half = own_ref.shape[1] // size
+        for k in range(2 * half):
+            for d, got_ref in enumerate((here_ref, there_ref)):
+                if k < half:
+                    part = own_ref.at[pl.ds(d * size, size), pl.ds(k * size, size)]
+                else:
+                    part = got_ref.at[:, pl.ds((k - half) * size, size)]
+                slot = where_ref[level, kind, d * 2 * half + k]
 
-            @pl.when(slot >= 0)
-            def _():
-                out_ref[:, cols] = held[jnp.maximum(slot, 0)]
+                @pl.when(slot >= 0)
+                def _():
+                    part[...] = held[jnp.maximum(slot, 0)]
 
-            @pl.when(slot < 0)
-            def _():
-                out_ref[:, cols] = jnp.zeros((size, size), out_ref.dtype)
+                @pl.when(slot < 0)
+                def _():
+                    part[...] = jnp.zeros((size, size), part.dtype)
 
 
 def build_tables(level, where, count, tiles):
     slots, size = tiles.shape[3:5]
-    out = jax.ShapeDtypeStruct((size, slots // 2 * size), tiles.dtype)
+    rows = (2 * size, size, size)
+    out = [jax.ShapeDtypeStruct((n, slots // 4 * size), tiles.dtype) for n in rows * 2]
     outs = pl.pallas_call(
         lambda *refs: table_kernel(level, *refs),
-        out_shape=[out] * 4,
+        out_shape=out,
         in_specs=[
             pl.BlockSpec(memory_space=pltpu.SMEM),
             pl.BlockSpec(memory_space=pltpu.SMEM),
-            pl.BlockSpec(memory_space=pl.ANY),
+            pl.BlockSpec(memory_space=pltpu.HBM),
         ],
-        out_specs=[pl.BlockSpec(memory_space=pltpu.VMEM)] * 4,
+        out_specs=[pl.BlockSpec(memory_space=pltpu.VMEM)] * 6,
         scratch_shapes=[pltpu.VMEM(tiles.shape[3:], tiles.dtype), pltpu.SemaphoreType.DMA],
         compiler_params=pltpu.CompilerParams(vmem_limit_bytes=VM << 20),
         cost_estimate=pl.CostEstimate(flops=0, bytes_accessed=12 << 20, transcendentals=0),
     )(where, count, tiles)
-    return {"y": outs[:2], "z": outs[2:]}
+    return {"y": outs[:3], "z": outs[3:]}
 
 
 def diagonal_solve(factor, values):
@@ -132,7 +138,7 @@
     orders = [gather_order(first, shape) for first in ("y", "z")]
 
     def body(rhs, tile_pairs, tiles, dinv):
-        levels = rhs.shape[0]
+        levels, size = rhs.shape[0], rhs.shape[3]
         rhs, dinv, pairs = rhs[:, 0, 0], dinv[:, 0, 0], tile_pairs[:, 0, 0]
         me = lax.axis_index("grid") * shape[1] + lax.axis_index("proc")
         held = jnp.stack([jnp.asarray(order)[me] for order in orders])
@@ -141,6 +147,7 @@
         index = lax.broadcasted_iota(jnp.int32, hit.shape, 3)
         where = jnp.max(jnp.where(hit, index, -1), -1)
         counts = jnp.sum((pairs >= 0).astype(jnp.int32), 1)
+        tiles = pltpu.with_memory_space_constraint(tiles, pltpu.HBM)
         tables = [build_tables(t, where, counts, tiles) for t in range(levels - 1)]
         solved = [[None] * len(CHUNKS) for _ in range(levels)]
         sent = [None] * len(CHUNKS)
@@ -150,11 +157,14 @@
         for level in range(1, levels):
             kind = LINK if level == levels - 1 else jnp.float32
             for c, (first, start, width) in enumerate(CHUNKS):
-                here, there = tables[level - 1][first]
-                blocks = gather_blocks(sent[c], first, shape)
-                away = jnp.dot(there, blocks, preferred_element_type=jnp.float32)
-                away = from_partner(away.astype(kind), shape, level - 1)
-                stay = jnp.dot(here, blocks, preferred_element_type=jnp.float32)
+                own, here, there = tables[level - 1][first]
+                held, got = gather_blocks(sent[c], first, shape)
+                part = jnp.dot(own, held, preferred_element_type=jnp.float32)
+                part = lax.optimization_barrier(part)
+                away = jnp.dot(there, got, preferred_element_type=jnp.float32)
+                away = (away + part[size:]).astype(kind)
+                away = from_partner(away, shape, level - 1)
+                stay = jnp.dot(here, got, preferred_element_type=jnp.float32) + part[:size]
                 stay = lax.optimization_barrier(
                     rhs[level, :, start : start + width] - stay
                 )
@@ -164,6 +174,7 @@
                     solved[level][c], sent[c] = now
                 else:
                     solved[level][c] = lax.optimization_barrier(now)
+        solved[0] = lax.optimization_barrier((solved[0], sent))[0]
         out = jnp.stack([jnp.concatenate(row, 1) for row in solved])[:, None, None]
         return out
 

time: 164 us -> 137 us (0.84)
  starting transfers between devices: 59.1 us -> 43.6 us
  waiting for transfers between devices: 48.7 us -> 61.4 us
  local copies, waits for them, and re-layouts: 11.1 us -> 0.72 us
  other arithmetic: 13.6 us -> 4 us
    ppermute x32, starting transfers between devices: 55.6 us -> 38.3 us  [gather_blocks(): got = lax.ppermute(held, AXES, exchange_route(shape, axis, step))]
    ppermute x32, waiting for transfers between devices: 42.4 us -> 54.4 us  [gather_blocks(): got = lax.ppermute(held, AXES, exchange_route(shape, axis, step))]
    unnamed x46 -> x6, local copies, waits for them, and re-layouts: 9.84 us -> 0.01 us
    concatenate x24, other arithmetic: 9.75 us -> 1.33 us  [gather_blocks(): held = lax.optimization_barrier(jnp.concatenate([held, got]))]
    dot_general x12, matrix products: 10.3 us -> 7.46 us  [diagonal_solve(): jnp.dot(factor, values, precision=lax.Precision.HIGH, preferred_element_t...]
    ppermute x8, starting transfers between devices: 3.43 us -> 5.33 us  [from_partner(): return lax.ppermute(block, AXES, route)]
    dot_general x16 -> x24, matrix products: 11.4 us -> 12.7 us  [the longest x8 5.69 us: body(): part = jnp.dot(own, held, preferred_element_type=jnp.float32)]
  transfers between devices with their start and end apart: 40 -> 40, of which waited for: 21 -> 20; matrix products, arithmetic and copies ran while one was open for 23% -> 15% of each run, Pallas kernels for 5% -> 5%
where the time goes in v1:
time: 137 us
  waiting for transfers between devices  61.4 us (45%)
  starting transfers between devices  43.6 us (32%)
  matrix products  20.1 us (15%)
  Pallas kernels  6.45 us (5%)
  other arithmetic  4 us (3%)
    ppermute x32, waiting for transfers between devices, gather_blocks(): got = lax.ppermute(held, AXES, exchange_route(shape, axis, step))  54.4 us
    ppermute x32, starting transfers between devices, gather_blocks(): got = lax.ppermute(held, AXES, exchange_route(shape, axis, step))  38.3 us
    dot_general x12, matrix products, diagonal_solve(): jnp.dot(factor, values, precision=lax.Precision.HIGH, preferred_element_t...  7.46 us
    ppermute x8, waiting for transfers between devices, from_partner(): return lax.ppermute(block, AXES, route)  6.98 us
    pallas_call x2, Pallas kernels, build_tables(): pl.pallas_call(lambda *refs: table_kernel(level, *refs), out_shape=out, i...  6.45 us
    dot_general x8, matrix products, body(): part = jnp.dot(own, held, preferred_element_type=jnp.float32)  5.69 us
    ppermute x8, starting transfers between devices, from_partner(): return lax.ppermute(block, AXES, route)  5.33 us
    dot_general x8, matrix products, body(): away = jnp.dot(there, got, preferred_element_type=jnp.float32)  3.5 us
  transfers between devices with their start and end apart: 40, of which 20 were waited for; matrix products, arithmetic and copies ran while one was open for 15% of the time, Pallas kernels for 5%

profile of v1, /device:TPU:0, one launch (start us, length us, event | category | flops | bytes accessed | tf_op | source)
XLA Modules:
  0.0 137.0 jit_solution(18117325304257185918)
XLA Ops:
  0.0 1.4 %fusion.59 = (bf16[256,256]{1,0:T(8,128)(2,1)S(1)}, f32[256,256]{1,0:T(8,128)S(1)}) fusion(f32[3,256,1024]{2,1,0:T(8,128)} %bitcast.211, f32[3,1,1,256,256]{4,3,2,1,0:T(8,128)} %param.9), kind=kOutput, calls=%fused_computation.129 | convolution fusion | flops 100728832 | bytes 917504 | tf_op jit(solution)/shard_map/dot_general | solution.py:132
  1.4 1.8 %collective-permute-start = (bf16[1,256,256]{2,1,0:T(8,128)(2,1)S(1)}, bf16[1,256,256]{2,1,0:T(8,128)(2,1)S(1)}, u32[]{:S(2)}, u32[]{:S(2)}) collective-permute-start(bf16[1,256,256]{2,1,0:T(8,128)(2,1)S(1)} %bitcast.237), channel_id=1, source_target_pairs={{0,1},{1,0},{2,3},{3,2},{4,5},{5,4},{6,7},{7,6},{8,9},{9,8},{10,11... | collective-permute-start | bytes 393224 | tf_op jit(solution)/shard_map/ppermute | solution.py:62
  3.2 1.3 fusion.57
  4.5 2.0 %collective-permute-start.5 = (bf16[1,256,256]{2,1,0:T(8,128)(2,1)S(1)}, bf16[1,256,256]{2,1,0:T(8,128)(2,1)S(1)}, u32[]{:S(2)}, u32[]{:S(2)}) collective-permute-start(bf16[1,256,256]{2,1,0:T(8,128)(2,1)S(1)} %bitcast.235), channel_id=1, source_target_pairs={{0,4},{1,5},{2,6},{3,7},{4,0},{5,1},{6,2},{7,3},{8,12},{9,13},{10,... | collective-permute-start | bytes 393224 | tf_op jit(solution)/shard_map/ppermute | solution.py:62
  10.5 3.2 %collective-permute-start.1 = (bf16[2,256,256]{2,1,0:T(8,128)(2,1)S(1)}, bf16[2,256,256]{2,1,0:T(8,128)(2,1)S(1)}, u32[]{:S(2)}, u32[]{:S(2)}) collective-permute-start(bf16[2,256,256]{2,1,0:T(8,128)(2,1)S(1)} %pad_maximum_fusion.16), channel_id=1, source_target_pairs={{0,3},{1,2},{2,1},{3,0},{4,7},{5,6},{6,5},{7,4},{8,11},{9,10},{10,... | collective-permute-start | bytes 786440 | tf_op jit(solution)/shard_map/ppermute | solution.py:62
  13.7 4.1 %collective-permute-start.6 = (bf16[2,256,256]{2,1,0:T(8,128)(2,1)S(1)}, bf16[2,256,256]{2,1,0:T(8,128)(2,1)S(1)}, u32[]{:S(2)}, u32[]{:S(2)}) collective-permute-start(bf16[2,256,256]{2,1,0:T(8,128)(2,1)S(1)} %pad_maximum_fusion.17), channel_id=1, source_target_pairs={{0,12},{1,13},{2,14},{3,15},{4,8},{5,9},{6,10},{7,11},{8,4},{9,5},... | collective-permute-start | bytes 786440 | tf_op jit(solution)/shard_map/ppermute | solution.py:62
  18.7 1.6 %collective-permute-start.2 = (bf16[4,256,256]{2,1,0:T(8,128)(2,1)S(1)}, bf16[4,256,256]{2,1,0:T(8,128)(2,1)S(1)}, u32[]{:S(2)}, u32[]{:S(2)}) collective-permute-start(bf16[4,256,256]{2,1,0:T(8,128)(2,1)S(1)} %pad_maximum_fusion.8), channel_id=1, source_target_pairs={{0,4},{1,5},{2,6},{3,7},{4,0},{5,1},{6,2},{7,3},{8,12},{9,13},{10,... | collective-permute-start | bytes 1572872 | tf_op jit(solution)/shard_map/ppermute | solution.py:62
  20.3 1.9 %collective-permute-done.6 = bf16[2,256,256]{2,1,0:T(8,128)(2,1)S(1)} collective-permute-done((bf16[2,256,256]{2,1,0:T(8,128)(2,1)S(1)}, bf16[2,256,256]{2,1,0:T(8,128)(2,1)S(1)}, u32[]{:S(2)}, u32[]{:S(2)}) %collective-permute-start.6) | collective-permute-done | bytes 262176 | tf_op jit(solution)/shard_map/ppermute | solution.py:62
  22.5 3.4 %collective-permute-done.11 = bf16[2,256,256]{2,1,0:T(8,128)(2,1)S(1)} collective-permute-done((bf16[2,256,256]{2,1,0:T(8,128)(2,1)S(1)}, bf16[2,256,256]{2,1,0:T(8,128)(2,1)S(1)}, u32[]{:S(2)}, u32[]{:S(2)}) %collective-permute-start.11) | collective-permute-done | bytes 262176 | tf_op jit(solution)/shard_map/ppermute | solution.py:62
  27.3 3.4 %shard_map.64 = (bf16[512,2048]{1,0:T(8,128)(2,1)S(1)}, bf16[256,2048]{1,0:T(8,128)(2,1)S(1)}, bf16[256,2048]{1,0:T(8,128)(2,1)S(1)}, bf16[512,2048]{1,0:T(8,128...) custom-call(s32[2,2,32]{2,1,0:T(2,128)S(1)} %select_reduce_fusion.refs_0_, ...), custom_call_target="tpu_custom_call" | custom-call | bytes 12582912 | tf_op jit(solution)/shard_map/pallas_call | solution.py:115
  30.7 3.0 %shard_map.65 = (bf16[512,2048]{1,0:T(8,128)(2,1)S(1)}, bf16[256,2048]{1,0:T(8,128)(2,1)S(1)}, bf16[256,2048]{1,0:T(8,128)(2,1)S(1)}, bf16[512,2048]{1,0:T(8,128...) custom-call(s32[2,2,32]{2,1,0:T(2,128)S(1)} %select_reduce_fusion.refs_0_, ...), custom_call_target="tpu_custom_call" | custom-call | bytes 12582912 | tf_op jit(solution)/shard_map/pallas_call | solution.py:115
  34.0 1.3 collective-permute-start.3
  35.4 1.5 %collective-permute-start.8 = (bf16[8,256,256]{2,1,0:T(8,128)(2,1)S(1)}, bf16[8,256,256]{2,1,0:T(8,128)(2,1)S(1)}, u32[]{:S(2)}, u32[]{:S(2)}) collective-permute-start(bf16[8,256,256]{2,1,0:T(8,128)(2,1)S(1)} %pad_maximum_fusion.1), channel_id=1, source_target_pairs={{0,3},{1,2},{2,1},{3,0},{4,7},{5,6},{6,5},{7,4},{8,11},{9,10},{10,... | collective-permute-start | bytes 3145736 | tf_op jit(solution)/shard_map/ppermute | solution.py:62
  39.9 8.7 %collective-permute-done.17 = bf16[4,256,256]{2,1,0:T(8,128)(2,1)S(1)} collective-permute-done((bf16[4,256,256]{2,1,0:T(8,128)(2,1)S(1)}, bf16[4,256,256]{2,1,0:T(8,128)(2,1)S(1)}, u32[]{:S(2)}, u32[]{:S(2)}) %collective-permute-start.17) | collective-permute-done | bytes 524320 | tf_op jit(solution)/shard_map/ppermute | solution.py:62
  52.0 1.5 %collective-permute-start.9 = (f32[256,256]{1,0:T(8,128)S(1)}, f32[256,256]{1,0:T(8,128)S(1)}, u32[]{:S(2)}, u32[]{:S(2)}) collective-permute-start(f32[256,256]{1,0:T(8,128)S(1)} %convolution_add_fusion.12), channel_id=1, source_target_pairs={{0,16},{1,17},{2,18},{3,19},{4,20},{5,21},{6,22},{7,23},{8,24},{9,... | collective-permute-start | bytes 786440 | tf_op jit(solution)/shard_map/ppermute | solution.py:70
  53.5 7.9 %collective-permute-done.13 = bf16[8,256,256]{2,1,0:T(8,128)(2,1)S(1)} collective-permute-done((bf16[8,256,256]{2,1,0:T(8,128)(2,1)S(1)}, bf16[8,256,256]{2,1,0:T(8,128)(2,1)S(1)}, u32[]{:S(2)}, u32[]{:S(2)}) %collective-permute-start.13) | collective-permute-done | bytes 1048608 | tf_op jit(solution)/shard_map/ppermute | solution.py:62
  63.1 1.9 %collective-permute-done.18 = bf16[8,256,256]{2,1,0:T(8,128)(2,1)S(1)} collective-permute-done((bf16[8,256,256]{2,1,0:T(8,128)(2,1)S(1)}, bf16[8,256,256]{2,1,0:T(8,128)(2,1)S(1)}, u32[]{:S(2)}, u32[]{:S(2)}) %collective-permute-start.18) | collective-permute-done | bytes 1048608 | tf_op jit(solution)/shard_map/ppermute | solution.py:62
  69.5 2.0 %collective-permute-start.30 = (bf16[1,256,256]{2,1,0:T(8,128)(2,1)S(1)}, bf16[1,256,256]{2,1,0:T(8,128)(2,1)S(1)}, u32[]{:S(2)}, u32[]{:S(2)}) collective-permute-start(bf16[1,256,256]{2,1,0:T(8,128)(2,1)S(1)} %bitcast.243), channel_id=1, source_target_pairs={{0,1},{1,0},{2,3},{3,2},{4,5},{5,4},{6,7},{7,6},{8,9},{9,8},{10,11... | collective-permute-start | bytes 393224 | tf_op jit(solution)/shard_map/ppermute | solution.py:62
  74.8 2.7 %collective-permute-start.31 = (bf16[2,256,256]{2,1,0:T(8,128)(2,1)S(1)}, bf16[2,256,256]{2,1,0:T(8,128)(2,1)S(1)}, u32[]{:S(2)}, u32[]{:S(2)}) collective-permute-start(bf16[2,256,256]{2,1,0:T(8,128)(2,1)S(1)} %pad_maximum_fusion.22), channel_id=1, source_target_pairs={{0,3},{1,2},{2,1},{3,0},{4,7},{5,6},{6,5},{7,4},{8,11},{9,10},{10,... | collective-permute-start | bytes 786440 | tf_op jit(solution)/shard_map/ppermute | solution.py:62
  77.5 3.1 %collective-permute-done.21 = bf16[2,256,256]{2,1,0:T(8,128)(2,1)S(1)} collective-permute-done((bf16[2,256,256]{2,1,0:T(8,128)(2,1)S(1)}, bf16[2,256,256]{2,1,0:T(8,128)(2,1)S(1)}, u32[]{:S(2)}, u32[]{:S(2)}) %collective-permute-start.21) | collective-permute-done | bytes 262176 | tf_op jit(solution)/shard_map/ppermute | solution.py:62
  80.6 1.3 collective-permute-start.22
  83.4 1.3 collective-permute-start.32
  84.9 7.6 %collective-permute-done.36 = bf16[2,256,256]{2,1,0:T(8,128)(2,1)S(1)} collective-permute-done((bf16[2,256,256]{2,1,0:T(8,128)(2,1)S(1)}, bf16[2,256,256]{2,1,0:T(8,128)(2,1)S(1)}, u32[]{:S(2)}, u32[]{:S(2)}) %collective-permute-start.36) | collective-permute-done | bytes 262176 | tf_op jit(solution)/shard_map/ppermute | solution.py:62
  94.6 5.3 %collective-permute-done.32 = bf16[4,256,256]{2,1,0:T(8,128)(2,1)S(1)} collective-permute-done((bf16[4,256,256]{2,1,0:T(8,128)(2,1)S(1)}, bf16[4,256,256]{2,1,0:T(8,128)(2,1)S(1)}, u32[]{:S(2)}, u32[]{:S(2)}) %collective-permute-start.32) | collective-permute-done | bytes 524320 | tf_op jit(solution)/shard_map/ppermute | solution.py:62
  100.0 3.5 %collective-permute-start.33 = (bf16[8,256,256]{2,1,0:T(8,128)(2,1)S(1)}, bf16[8,256,256]{2,1,0:T(8,128)(2,1)S(1)}, u32[]{:S(2)}, u32[]{:S(2)}) collective-permute-start(bf16[8,256,256]{2,1,0:T(8,128)(2,1)S(1)} %pad_maximum_fusion.6), channel_id=1, source_target_pairs={{0,12},{1,13},{2,14},{3,15},{4,8},{5,9},{6,10},{7,11},{8,4},{9,5},... | collective-permute-start | bytes 3145736 | tf_op jit(solution)/shard_map/ppermute | solution.py:62
  105.6 1.8 %collective-permute-done.37 = bf16[4,256,256]{2,1,0:T(8,128)(2,1)S(1)} collective-permute-done((bf16[4,256,256]{2,1,0:T(8,128)(2,1)S(1)}, bf16[4,256,256]{2,1,0:T(8,128)(2,1)S(1)}, u32[]{:S(2)}, u32[]{:S(2)}) %collective-permute-start.37) | collective-permute-done | bytes 524320 | tf_op jit(solution)/shard_map/ppermute | solution.py:62
  107.5 1.7 %collective-permute-start.38 = (bf16[8,256,256]{2,1,0:T(8,128)(2,1)S(1)}, bf16[8,256,256]{2,1,0:T(8,128)(2,1)S(1)}, u32[]{:S(2)}, u32[]{:S(2)}) collective-permute-start(bf16[8,256,256]{2,1,0:T(8,128)(2,1)S(1)} %pad_maximum_fusion.7), channel_id=1, source_target_pairs={{0,3},{1,2},{2,1},{3,0},{4,7},{5,6},{6,5},{7,4},{8,11},{9,10},{10,... | collective-permute-start | bytes 3145736 | tf_op jit(solution)/shard_map/ppermute | solution.py:62
  110.8 9.2 %collective-permute-done.33 = bf16[8,256,256]{2,1,0:T(8,128)(2,1)S(1)} collective-permute-done((bf16[8,256,256]{2,1,0:T(8,128)(2,1)S(1)}, bf16[8,256,256]{2,1,0:T(8,128)(2,1)S(1)}, u32[]{:S(2)}, u32[]{:S(2)}) %collective-permute-start.33) | collective-permute-done | bytes 1048608 | tf_op jit(solution)/shard_map/ppermute | solution.py:62
  125.2 1.4 %collective-permute-start.34 = (bf16[256,256]{1,0:T(8,128)(2,1)S(1)}, bf16[256,256]{1,0:T(8,128)(2,1)S(1)}, u32[]{:S(2)}, u32[]{:S(2)}) collective-permute-start(bf16[256,256]{1,0:T(8,128)(2,1)S(1)} %fusion.10), channel_id=1, source_target_pairs={{0,32},{1,33},{2,34},{3,35},{4,36},{5,37},{6,38},{7,39},{8,40},{9,... | collective-permute-start | bytes 393224 | tf_op jit(solution)/shard_map/ppermute | solution.py:70
  127.5 3.4 %collective-permute-done.29 = bf16[256,256]{1,0:T(8,128)(2,1)S(1)} collective-permute-done((bf16[256,256]{1,0:T(8,128)(2,1)S(1)}, bf16[256,256]{1,0:T(8,128)(2,1)S(1)}, u32[]{:S(2)}, u32[]{:S(2)}) %collective-permute-start.29) | collective-permute-done | bytes 131104 | tf_op jit(solution)/shard_map/ppermute | solution.py:70
  131.2 2.0 %collective-permute-done.34 = bf16[256,256]{1,0:T(8,128)(2,1)S(1)} collective-permute-done((bf16[256,256]{1,0:T(8,128)(2,1)S(1)}, bf16[256,256]{1,0:T(8,128)(2,1)S(1)}, u32[]{:S(2)}, u32[]{:S(2)}) %collective-permute-start.34) | collective-permute-done | bytes 131104 | tf_op jit(solution)/shard_map/ppermute | solution.py:70
  135.1 1.9 %maximum_bitcast_fusion = f32[3,1,1,256,1024]{4,3,2,1,0:T(8,128)} fusion(f32[1,256,1024]{2,1,0:T(8,128)S(1)} %maximum_bitcast_fusion.3, f32[1,256,1024]{2,1,0:T(8,128)S(1)} %maximum_bitcast_fusion.2, f32[1,256,1024]{2,1,0:T(8,128)S(1)} %maximum_bitcast_fusion.1), kind=kLoop, calls=%fused_computation | loop fusion | flops 1572864 | bytes 6291456 | tf_op jit(solution)/shard_map/broadcast_in_dim | solution.py:178
  (125 shorter events, 38.4 us)
Async XLA Ops:
  1.4 9.1 %collective-permute-start = (bf16[1,256,256]{2,1,0:T(8,128)(2,1)S(1)}, bf16[1,256,256]{2,1,0:T(8,128)(2,1)S(1)}, u32[]{:S(2)}, u32[]{:S(2)}) collective-permute-start(bf16[1,256,256]{2,1,0:T(8,128)(2,1)S(1)} %bitcast.237), channel_id=1, source_target_pairs={{0,1},{1,0},{2,3},{3,2},{4,5},{5,4},{6,7},{7,6},{8,9},{9,8},{10,11... | collective-permute-start | bytes 393224 | tf_op jit(solution)/shard_map/ppermute | solution.py:62
  4.5 9.2 %collective-permute-start.5 = (bf16[1,256,256]{2,1,0:T(8,128)(2,1)S(1)}, bf16[1,256,256]{2,1,0:T(8,128)(2,1)S(1)}, u32[]{:S(2)}, u32[]{:S(2)}) collective-permute-start(bf16[1,256,256]{2,1,0:T(8,128)(2,1)S(1)} %bitcast.235), channel_id=1, source_target_pairs={{0,4},{1,5},{2,6},{3,7},{4,0},{5,1},{6,2},{7,3},{8,12},{9,13},{10,... | collective-permute-start | bytes 393224 | tf_op jit(solution)/shard_map/ppermute | solution.py:62
  7.8 10.1 %collective-permute-start.10 = (bf16[1,256,256]{2,1,0:T(8,128)(2,1)S(1)}, bf16[1,256,256]{2,1,0:T(8,128)(2,1)S(1)}, u32[]{:S(2)}, u32[]{:S(2)}) collective-permute-start(bf16[1,256,256]{2,1,0:T(8,128)(2,1)S(1)} %bitcast.233), channel_id=1, source_target_pairs={{0,1},{1,0},{2,3},{3,2},{4,5},{5,4},{6,7},{7,6},{8,9},{9,8},{10,11... | collective-permute-start | bytes 393224 | tf_op jit(solution)/shard_map/ppermute | solution.py:62
  9.5 8.7 %collective-permute-start.15 = (bf16[1,256,256]{2,1,0:T(8,128)(2,1)S(1)}, bf16[1,256,256]{2,1,0:T(8,128)(2,1)S(1)}, u32[]{:S(2)}, u32[]{:S(2)}) collective-permute-start(bf16[1,256,256]{2,1,0:T(8,128)(2,1)S(1)} %bitcast.231), channel_id=1, source_target_pairs={{0,4},{1,5},{2,6},{3,7},{4,0},{5,1},{6,2},{7,3},{8,12},{9,13},{10,... | collective-permute-start | bytes 393224 | tf_op jit(solution)/shard_map/ppermute | solution.py:62
  10.5 8.2 %collective-permute-start.1 = (bf16[2,256,256]{2,1,0:T(8,128)(2,1)S(1)}, bf16[2,256,256]{2,1,0:T(8,128)(2,1)S(1)}, u32[]{:S(2)}, u32[]{:S(2)}) collective-permute-start(bf16[2,256,256]{2,1,0:T(8,128)(2,1)S(1)} %pad_maximum_fusion.16), channel_id=1, source_target_pairs={{0,3},{1,2},{2,1},{3,0},{4,7},{5,6},{6,5},{7,4},{8,11},{9,10},{10,... | collective-permute-start | bytes 786440 | tf_op jit(solution)/shard_map/ppermute | solution.py:62
  13.7 8.5 %collective-permute-start.6 = (bf16[2,256,256]{2,1,0:T(8,128)(2,1)S(1)}, bf16[2,256,256]{2,1,0:T(8,128)(2,1)S(1)}, u32[]{:S(2)}, u32[]{:S(2)}) collective-permute-start(bf16[2,256,256]{2,1,0:T(8,128)(2,1)S(1)} %pad_maximum_fusion.17), channel_id=1, source_target_pairs={{0,12},{1,13},{2,14},{3,15},{4,8},{5,9},{6,10},{7,11},{8,4},{9,5},... | collective-permute-start | bytes 786440 | tf_op jit(solution)/shard_map/ppermute | solution.py:62
  18.2 15.5 %collective-permute-start.16 = (bf16[2,256,256]{2,1,0:T(8,128)(2,1)S(1)}, bf16[2,256,256]{2,1,0:T(8,128)(2,1)S(1)}, u32[]{:S(2)}, u32[]{:S(2)}) collective-permute-start(bf16[2,256,256]{2,1,0:T(8,128)(2,1)S(1)} %pad_maximum_fusion.19), channel_id=1, source_target_pairs={{0,12},{1,13},{2,14},{3,15},{4,8},{5,9},{6,10},{7,11},{8,4},{9,5},... | collective-permute-start | bytes 786440 | tf_op jit(solution)/shard_map/ppermute | solution.py:62
  18.7 15.1 %collective-permute-start.2 = (bf16[4,256,256]{2,1,0:T(8,128)(2,1)S(1)}, bf16[4,256,256]{2,1,0:T(8,128)(2,1)S(1)}, u32[]{:S(2)}, u32[]{:S(2)}) collective-permute-start(bf16[4,256,256]{2,1,0:T(8,128)(2,1)S(1)} %pad_maximum_fusion.8), channel_id=1, source_target_pairs={{0,4},{1,5},{2,6},{3,7},{4,0},{5,1},{6,2},{7,3},{8,12},{9,13},{10,... | collective-permute-start | bytes 1572872 | tf_op jit(solution)/shard_map/ppermute | solution.py:62
  22.3 13.1 %collective-permute-start.7 = (bf16[4,256,256]{2,1,0:T(8,128)(2,1)S(1)}, bf16[4,256,256]{2,1,0:T(8,128)(2,1)S(1)}, u32[]{:S(2)}, u32[]{:S(2)}) collective-permute-start(bf16[4,256,256]{2,1,0:T(8,128)(2,1)S(1)} %pad_maximum_fusion.9), channel_id=1, source_target_pairs={{0,1},{1,0},{2,3},{3,2},{4,5},{5,4},{6,7},{7,6},{8,9},{9,8},{10,11... | collective-permute-start | bytes 1572872 | tf_op jit(solution)/shard_map/ppermute | solution.py:62
  25.9 11.1 %collective-permute-start.12 = (bf16[4,256,256]{2,1,0:T(8,128)(2,1)S(1)}, bf16[4,256,256]{2,1,0:T(8,128)(2,1)S(1)}, u32[]{:S(2)}, u32[]{:S(2)}) collective-permute-start(bf16[4,256,256]{2,1,0:T(8,128)(2,1)S(1)} %pad_maximum_fusion.10), channel_id=1, source_target_pairs={{0,4},{1,5},{2,6},{3,7},{4,0},{5,1},{6,2},{7,3},{8,12},{9,13},{10,... | collective-permute-start | bytes 1572872 | tf_op jit(solution)/shard_map/ppermute | solution.py:62
  33.8 14.9 %collective-permute-start.17 = (bf16[4,256,256]{2,1,0:T(8,128)(2,1)S(1)}, bf16[4,256,256]{2,1,0:T(8,128)(2,1)S(1)}, u32[]{:S(2)}, u32[]{:S(2)}) collective-permute-start(bf16[4,256,256]{2,1,0:T(8,128)(2,1)S(1)} %pad_maximum_fusion.11), channel_id=1, source_target_pairs={{0,1},{1,0},{2,3},{3,2},{4,5},{5,4},{6,7},{7,6},{8,9},{9,8},{10,11... | collective-permute-start | bytes 1572872 | tf_op jit(solution)/shard_map/ppermute | solution.py:62
  34.0 16.1 %collective-permute-start.3 = (bf16[8,256,256]{2,1,0:T(8,128)(2,1)S(1)}, bf16[8,256,256]{2,1,0:T(8,128)(2,1)S(1)}, u32[]{:S(2)}, u32[]{:S(2)}) collective-permute-start(bf16[8,256,256]{2,1,0:T(8,128)(2,1)S(1)} %pad_maximum_fusion), channel_id=1, source_target_pairs={{0,12},{1,13},{2,14},{3,15},{4,8},{5,9},{6,10},{7,11},{8,4},{9,5},... | collective-permute-start | bytes 3145736 | tf_op jit(solution)/shard_map/ppermute | solution.py:62
  35.4 16.1 %collective-permute-start.8 = (bf16[8,256,256]{2,1,0:T(8,128)(2,1)S(1)}, bf16[8,256,256]{2,1,0:T(8,128)(2,1)S(1)}, u32[]{:S(2)}, u32[]{:S(2)}) collective-permute-start(bf16[8,256,256]{2,1,0:T(8,128)(2,1)S(1)} %pad_maximum_fusion.1), channel_id=1, source_target_pairs={{0,3},{1,2},{2,1},{3,0},{4,7},{5,6},{6,5},{7,4},{8,11},{9,10},{10,... | collective-permute-start | bytes 3145736 | tf_op jit(solution)/shard_map/ppermute | solution.py:62
  37.0 24.3 %collective-permute-start.13 = (bf16[8,256,256]{2,1,0:T(8,128)(2,1)S(1)}, bf16[8,256,256]{2,1,0:T(8,128)(2,1)S(1)}, u32[]{:S(2)}, u32[]{:S(2)}) collective-permute-start(bf16[8,256,256]{2,1,0:T(8,128)(2,1)S(1)} %pad_maximum_fusion.2), channel_id=1, source_target_pairs={{0,12},{1,13},{2,14},{3,15},{4,8},{5,9},{6,10},{7,11},{8,4},{9,5},... | collective-permute-start | bytes 3145736 | tf_op jit(solution)/shard_map/ppermute | solution.py:62
  48.8 16.3 %collective-permute-start.18 = (bf16[8,256,256]{2,1,0:T(8,128)(2,1)S(1)}, bf16[8,256,256]{2,1,0:T(8,128)(2,1)S(1)}, u32[]{:S(2)}, u32[]{:S(2)}) collective-permute-start(bf16[8,256,256]{2,1,0:T(8,128)(2,1)S(1)} %pad_maximum_fusion.3), channel_id=1, source_target_pairs={{0,3},{1,2},{2,1},{3,0},{4,7},{5,6},{6,5},{7,4},{8,11},{9,10},{10,... | collective-permute-start | bytes 3145736 | tf_op jit(solution)/shard_map/ppermute | solution.py:62
  50.5 16.0 %collective-permute-start.4 = (f32[256,256]{1,0:T(8,128)S(1)}, f32[256,256]{1,0:T(8,128)S(1)}, u32[]{:S(2)}, u32[]{:S(2)}) collective-permute-start(f32[256,256]{1,0:T(8,128)S(1)} %convolution_add_fusion.14), channel_id=1, source_target_pairs={{0,16},{1,17},{2,18},{3,19},{4,20},{5,21},{6,22},{7,23},{8,24},{9,... | collective-permute-start | bytes 786440 | tf_op jit(solution)/shard_map/ppermute | solution.py:70
  52.0 14.8 %collective-permute-start.9 = (f32[256,256]{1,0:T(8,128)S(1)}, f32[256,256]{1,0:T(8,128)S(1)}, u32[]{:S(2)}, u32[]{:S(2)}) collective-permute-start(f32[256,256]{1,0:T(8,128)S(1)} %convolution_add_fusion.12), channel_id=1, source_target_pairs={{0,16},{1,17},{2,18},{3,19},{4,20},{5,21},{6,22},{7,23},{8,24},{9,... | collective-permute-start | bytes 786440 | tf_op jit(solution)/shard_map/ppermute | solution.py:70
  71.6 10.4 %collective-permute-start.35 = (bf16[1,256,256]{2,1,0:T(8,128)(2,1)S(1)}, bf16[1,256,256]{2,1,0:T(8,128)(2,1)S(1)}, u32[]{:S(2)}, u32[]{:S(2)}) collective-permute-start(bf16[1,256,256]{2,1,0:T(8,128)(2,1)S(1)} %bitcast.239), channel_id=1, source_target_pairs={{0,4},{1,5},{2,6},{3,7},{4,0},{5,1},{6,2},{7,3},{8,12},{9,13},{10,... | collective-permute-start | bytes 393224 | tf_op jit(solution)/shard_map/ppermute | solution.py:62
  73.5 8.5 %collective-permute-start.26 = (bf16[2,256,256]{2,1,0:T(8,128)(2,1)S(1)}, bf16[2,256,256]{2,1,0:T(8,128)(2,1)S(1)}, u32[]{:S(2)}, u32[]{:S(2)}) collective-permute-start(bf16[2,256,256]{2,1,0:T(8,128)(2,1)S(1)} %pad_maximum_fusion.21), channel_id=1, source_target_pairs={{0,12},{1,13},{2,14},{3,15},{4,8},{5,9},{6,10},{7,11},{8,4},{9,5},... | collective-permute-start | bytes 786440 | tf_op jit(solution)/shard_map/ppermute | solution.py:62
  74.8 8.6 %collective-permute-start.31 = (bf16[2,256,256]{2,1,0:T(8,128)(2,1)S(1)}, bf16[2,256,256]{2,1,0:T(8,128)(2,1)S(1)}, u32[]{:S(2)}, u32[]{:S(2)}) collective-permute-start(bf16[2,256,256]{2,1,0:T(8,128)(2,1)S(1)} %pad_maximum_fusion.22), channel_id=1, source_target_pairs={{0,3},{1,2},{2,1},{3,0},{4,7},{5,6},{6,5},{7,4},{8,11},{9,10},{10,... | collective-permute-start | bytes 786440 | tf_op jit(solution)/shard_map/ppermute | solution.py:62
  80.6 12.0 %collective-permute-start.22 = (bf16[4,256,256]{2,1,0:T(8,128)(2,1)S(1)}, bf16[4,256,256]{2,1,0:T(8,128)(2,1)S(1)}, u32[]{:S(2)}, u32[]{:S(2)}) collective-permute-start(bf16[4,256,256]{2,1,0:T(8,128)(2,1)S(1)} %pad_maximum_fusion.12), channel_id=1, source_target_pairs={{0,4},{1,5},{2,6},{3,7},{4,0},{5,1},{6,2},{7,3},{8,12},{9,13},{10,... | collective-permute-start | bytes 1572872 | tf_op jit(solution)/shard_map/ppermute | solution.py:62
  82.0 10.5 %collective-permute-start.36 = (bf16[2,256,256]{2,1,0:T(8,128)(2,1)S(1)}, bf16[2,256,256]{2,1,0:T(8,128)(2,1)S(1)}, u32[]{:S(2)}, u32[]{:S(2)}) collective-permute-start(bf16[2,256,256]{2,1,0:T(8,128)(2,1)S(1)} %pad_maximum_fusion.23), channel_id=1, source_target_pairs={{0,12},{1,13},{2,14},{3,15},{4,8},{5,9},{6,10},{7,11},{8,4},{9,5},... | collective-permute-start | bytes 786440 | tf_op jit(solution)/shard_map/ppermute | solution.py:62
  82.1 11.6 %collective-permute-start.27 = (bf16[4,256,256]{2,1,0:T(8,128)(2,1)S(1)}, bf16[4,256,256]{2,1,0:T(8,128)(2,1)S(1)}, u32[]{:S(2)}, u32[]{:S(2)}) collective-permute-start(bf16[4,256,256]{2,1,0:T(8,128)(2,1)S(1)} %pad_maximum_fusion.13), channel_id=1, source_target_pairs={{0,1},{1,0},{2,3},{3,2},{4,5},{5,4},{6,7},{7,6},{8,9},{9,8},{10,11... | collective-permute-start | bytes 1572872 | tf_op jit(solution)/shard_map/ppermute | solution.py:62
  83.4 16.5 %collective-permute-start.32 = (bf16[4,256,256]{2,1,0:T(8,128)(2,1)S(1)}, bf16[4,256,256]{2,1,0:T(8,128)(2,1)S(1)}, u32[]{:S(2)}, u32[]{:S(2)}) collective-permute-start(bf16[4,256,256]{2,1,0:T(8,128)(2,1)S(1)} %pad_maximum_fusion.14), channel_id=1, source_target_pairs={{0,4},{1,5},{2,6},{3,7},{4,0},{5,1},{6,2},{7,3},{8,12},{9,13},{10,... | collective-permute-start | bytes 1572872 | tf_op jit(solution)/shard_map/ppermute | solution.py:62
  92.5 14.9 %collective-permute-start.37 = (bf16[4,256,256]{2,1,0:T(8,128)(2,1)S(1)}, bf16[4,256,256]{2,1,0:T(8,128)(2,1)S(1)}, u32[]{:S(2)}, u32[]{:S(2)}) collective-permute-start(bf16[4,256,256]{2,1,0:T(8,128)(2,1)S(1)} %pad_maximum_fusion.15), channel_id=1, source_target_pairs={{0,1},{1,0},{2,3},{3,2},{4,5},{5,4},{6,7},{7,6},{8,9},{9,8},{10,11... | collective-permute-start | bytes 1572872 | tf_op jit(solution)/shard_map/ppermute | solution.py:62
  92.7 17.2 %collective-permute-start.23 = (bf16[8,256,256]{2,1,0:T(8,128)(2,1)S(1)}, bf16[8,256,256]{2,1,0:T(8,128)(2,1)S(1)}, u32[]{:S(2)}, u32[]{:S(2)}) collective-permute-start(bf16[8,256,256]{2,1,0:T(8,128)(2,1)S(1)} %pad_maximum_fusion.4), channel_id=1, source_target_pairs={{0,12},{1,13},{2,14},{3,15},{4,8},{5,9},{6,10},{7,11},{8,4},{9,5},... | collective-permute-start | bytes 3145736 | tf_op jit(solution)/shard_map/ppermute | solution.py:62
  93.9 26.6 %collective-permute-start.28 = (bf16[8,256,256]{2,1,0:T(8,128)(2,1)S(1)}, bf16[8,256,256]{2,1,0:T(8,128)(2,1)S(1)}, u32[]{:S(2)}, u32[]{:S(2)}) collective-permute-start(bf16[8,256,256]{2,1,0:T(8,128)(2,1)S(1)} %pad_maximum_fusion.5), channel_id=1, source_target_pairs={{0,3},{1,2},{2,1},{3,0},{4,7},{5,6},{6,5},{7,4},{8,11},{9,10},{10,... | collective-permute-start | bytes 3145736 | tf_op jit(solution)/shard_map/ppermute | solution.py:62
  100.0 20.1 %collective-permute-start.33 = (bf16[8,256,256]{2,1,0:T(8,128)(2,1)S(1)}, bf16[8,256,256]{2,1,0:T(8,128)(2,1)S(1)}, u32[]{:S(2)}, u32[]{:S(2)}) collective-permute-start(bf16[8,256,256]{2,1,0:T(8,128)(2,1)S(1)} %pad_maximum_fusion.6), channel_id=1, source_target_pairs={{0,12},{1,13},{2,14},{3,15},{4,8},{5,9},{6,10},{7,11},{8,4},{9,5},... | collective-permute-start | bytes 3145736 | tf_op jit(solution)/shard_map/ppermute | solution.py:62
  107.5 16.1 %collective-permute-start.38 = (bf16[8,256,256]{2,1,0:T(8,128)(2,1)S(1)}, bf16[8,256,256]{2,1,0:T(8,128)(2,1)S(1)}, u32[]{:S(2)}, u32[]{:S(2)}) collective-permute-start(bf16[8,256,256]{2,1,0:T(8,128)(2,1)S(1)} %pad_maximum_fusion.7), channel_id=1, source_target_pairs={{0,3},{1,2},{2,1},{3,0},{4,7},{5,6},{6,5},{7,4},{8,11},{9,10},{10,... | collective-permute-start | bytes 3145736 | tf_op jit(solution)/shard_map/ppermute | solution.py:62
  110.4 16.9 %collective-permute-start.24 = (bf16[256,256]{1,0:T(8,128)(2,1)S(1)}, bf16[256,256]{1,0:T(8,128)(2,1)S(1)}, u32[]{:S(2)}, u32[]{:S(2)}) collective-permute-start(bf16[256,256]{1,0:T(8,128)(2,1)S(1)} %fusion.8), channel_id=1, source_target_pairs={{0,32},{1,33},{2,34},{3,35},{4,36},{5,37},{6,38},{7,39},{8,40},{9,... | collective-permute-start | bytes 393224 | tf_op jit(solution)/shard_map/ppermute | solution.py:70
  125.2 8.0 %collective-permute-start.34 = (bf16[256,256]{1,0:T(8,128)(2,1)S(1)}, bf16[256,256]{1,0:T(8,128)(2,1)S(1)}, u32[]{:S(2)}, u32[]{:S(2)}) collective-permute-start(bf16[256,256]{1,0:T(8,128)(2,1)S(1)} %fusion.10), channel_id=1, source_target_pairs={{0,32},{1,33},{2,34},{3,35},{4,36},{5,37},{6,38},{7,39},{8,40},{9,... | collective-permute-start | bytes 393224 | tf_op jit(solution)/shard_map/ppermute | solution.py:70
  126.6 8.1 %collective-permute-start.39 = (bf16[256,256]{1,0:T(8,128)(2,1)S(1)}, bf16[256,256]{1,0:T(8,128)(2,1)S(1)}, u32[]{:S(2)}, u32[]{:S(2)}) collective-permute-start(bf16[256,256]{1,0:T(8,128)(2,1)S(1)} %fusion.11), channel_id=1, source_target_pairs={{0,32},{1,33},{2,34},{3,35},{4,36},{5,37},{6,38},{7,39},{8,40},{9,... | collective-permute-start | bytes 393224 | tf_op jit(solution)/shard_map/ppermute | solution.py:70
  (11 other events, 69.3 us)
